TPU v7x, 32 devices: a whole 2x2x4 slice. The times are simulated.
32 devices in a mesh: req: 8 (over y, x, core), cand: 4 (over z).
Axes of the slice: x: 2, y: 2, z: 4, core: 2. Of those that a mesh axis runs over, the one named last changes fastest.
Arguments:
- history: bfloat16 [64, 256, 1024], P('req', 'cand'), may hold values from -6 to 6
- history_length: int32 [64], P('req'), may hold values from 32 to 256
- candidate_count: int32 [64], P('req'), may hold values from 512 to 4096
- block_shard: int32 [64, 32], P('req'), may hold values from 0 to 3, as said below
- block_index: int32 [64, 32], P('req'), may hold values from 0 to 3
- item_table: bfloat16 [16, 128, 1024], P('cand'), may hold values from -6 to 6
- item_ages: int32 [64, 4096], P('req', 'cand'), may hold values from 0 to 336
- history_weight: bfloat16 [1024, 2048], P('req'), may hold values from -0.1875 to 0.1875
- candidate_weight: bfloat16 [1024, 2048], P('req'), may hold values from -0.1875 to 0.1875
- output_weight: bfloat16 [1024, 1024], P('req'), may hold values from -0.1875 to 0.1875
- hidden_weight: bfloat16 [1024, 256], P('req'), may hold values from -0.1875 to 0.1875
- norm_gain: float32 [1024], replicated, may hold values from 0.1 to 1.9
- score_weight: bfloat16 [2, 256], replicated, may hold values from -0.375 to 0.375
Outputs:
- scores: float32 [64, 4096], P('req', 'cand')
Inputs may be any that keep to these rules, and one draw needn't show every extreme that they name: `block_shard`: for each group of 8 consecutive requests (aligned) and each c, the slots j with j // 8 == c of those requests name every shard exactly 16 times.
All inputs are finite; a program needn't handle non-finite values.
Results may differ from a plain program's by a relative error of at most 0.0053.
Values may be sent and summed in bfloat16 or wider, within the bound.
A program may use at most 128 MiB of HBM per device.

v0:
```python
import functools
import math

import jax
import jax.numpy as jnp
from jax import lax
from jax.experimental import pallas as pl
from jax.experimental.pallas import tpu as pltpu
from jax.sharding import PartitionSpec as P

HEADS = 8
BLOCK = 128
EPSILON = 1e-05
AGE_SCALE = 48.0


def silu(value):
    half = 0.5 * value
    return half + half * jnp.tanh(half)


MESH = pl.DeviceIdType.MESH


def pair_kernel(
    groups,
    shards,
    length_ref,
    history_ref,
    items_ref,
    history_shard_ref,
    candidate_shard_ref,
    output_shard_ref,
    hidden_shard_ref,
    gain_ref,
    score_weight_ref,
    logits_ref,
    events_ref,
    history_weight_ref,
    candidate_weight_ref,
    output_weight_ref,
    hidden_weight_ref,
    query_ref,
    gate_ref,
    pairs_ref,
    attended_ref,
    weight_send,
    weight_recv,
    pass_send,
    turn_send,
    event_send,
    event_recv,
    logit_send,
    logit_recv,
    own_sem,
):
    group = lax.axis_index("req")
    shard = lax.axis_index("cand")
    partner = group + 1 - 2 * lax.rem(group, 2)
    requests, own_events, width = history_ref.shape
    history_total = events_ref.shape[1]
    head = width // HEADS
    half_scale = 0.5 / math.sqrt(head)
    weights = (
        (candidate_shard_ref, candidate_weight_ref),
        (history_shard_ref, history_weight_ref),
        (output_shard_ref, output_weight_ref),
        (hidden_shard_ref, hidden_weight_ref),
    )
    depth = history_shard_ref.shape[0]
    half = groups // 2
    row, core = lax.div(group, half), lax.rem(group, 2)
    across = lax.rem(group + half, groups)
    beside = [row * half + lax.rem(group - row * half + 2 * d, half) for d in range(1, half // 2)]
    diagonal = [lax.rem(source + half, groups) for source in beside]
    near = (*beside, across)
    same_core = (*near, *diagonal)
    partner_core = [source + partner - group for source in same_core]
    others = [lax.rem(shard + d, shards) for d in range(1, shards)]
    last = shards - 1
    relays = ((1, last, 0), (last - 1, 0, last)) if shards > 2 else ()
    lead = requests // 2
    ahead = lead // 2

    def rows_of(source):
        return pl.ds(pl.multiple_of(source * depth, depth), depth)

    def events_of(source):
        return pl.ds(pl.multiple_of(source * own_events, own_events), own_events)

    def weight_copy(w, target, source, send):
        part, full = weights[w]
        return pltpu.make_async_remote_copy(
            src_ref=part,
            dst_ref=full.at[rows_of(source)],
            send_sem=send,
            recv_sem=weight_recv.at[w, source],
            device_id={"req": target},
            device_id_type=MESH,
        )

    def pass_copy(w, k, source):
        full = weights[w][1]
        return pltpu.make_async_remote_copy(
            src_ref=full.at[rows_of(source)],
            dst_ref=full.at[rows_of(source)],
            send_sem=pass_send.at[w, k],
            recv_sem=weight_recv.at[w, source],
            device_id={"req": partner},
            device_id_type=MESH,
        )

    def turn_copy(w, k):
        full = weights[w][1]
        source = beside[k] + core * (across - beside[k])
        target = across + core * (beside[k] - across)
        return pltpu.make_async_remote_copy(
            src_ref=full.at[rows_of(source)],
            dst_ref=full.at[rows_of(source)],
            send_sem=turn_send.at[w, k],
            recv_sem=weight_recv.at[w, source],
            device_id={"req": target},
            device_id_type=MESH,
        )

    def relay_copy(i, k):
        _, source, target = relays[k]
        return pltpu.make_async_remote_copy(
            src_ref=events_ref.at[i, events_of(source)],
            dst_ref=events_ref.at[i, events_of(source)],
            send_sem=event_send.at[i, len(others) + k],
            recv_sem=event_recv.at[i, source],
            device_id={"cand": target},
            device_id_type=MESH,
        )

    def is_far(target):
        return (shards > 2) & (jnp.abs(target - shard) == last)

    def is_relayed(source):
        flag = shard < 0
        for middle, start, _ in relays:
            flag = flag | ((shard == middle) & (source == start))
        return flag

    def relay(i):
        for k, (middle, source, _) in enumerate(relays):

            @pl.when(shard == middle)
            def _():
                event_copy(i, 0, 0, source).wait_recv()
                relay_copy(i, k).start()

    def event_copy(i, k, target, source):
        return pltpu.make_async_remote_copy(
            src_ref=history_ref.at[i],
            dst_ref=events_ref.at[i, events_of(source)],
            send_sem=event_send.at[i, k],
            recv_sem=event_recv.at[i, source],
            device_id={"cand": target},
            device_id_type=MESH,
        )

    def logit_copy(i, k, target, source):
        return pltpu.make_async_remote_copy(
            src_ref=logits_ref.at[source, i],
            dst_ref=logits_ref.at[source, i],
            send_sem=logit_send.at[i, k],
            recv_sem=logit_recv.at[i, source],
            device_id={"cand": target},
            device_id_type=MESH,
        )

    def own_weight(w):
        part, full = weights[w]
        return pltpu.make_async_copy(part, full.at[rows_of(group)], own_sem.at[w])

    def own_event(i):
        return pltpu.make_async_copy(
            history_ref.at[i], events_ref.at[i, events_of(shard)], own_sem.at[len(weights) + i]
        )

    barrier = pltpu.get_barrier_semaphore()
    for target in (*near, partner):
        pl.semaphore_signal(barrier, inc=1, device_id={"req": target}, device_id_type=MESH)
    for target in others:
        pl.semaphore_signal(barrier, inc=1, device_id={"cand": target}, device_id_type=MESH)
    pl.semaphore_wait(barrier, len(near) + 1 + len(others))

    def send(w):
        for k, target in enumerate((*near, partner)):
            weight_copy(w, target, group, weight_send.at[w, k]).start()
        own_weight(w).start()

    send(0)
    send(1)

    @pl.loop(0, requests)
    def _(i):
        for k, target in enumerate(others):

            @pl.when(jnp.logical_not(is_far(target)))
            def _():
                event_copy(i, k, target, shard).start()

        own_event(i).start()

    def pass_on(w, sources, first):
        for k, source in enumerate(sources):
            pass_copy(w, first + k, source).start()

    def arrive(w, sources):
        for source in sources:
            weight_copy(w, partner, source, weight_send.at[w, 0]).wait_recv()

    def turn(w):
        arrive(w, near)
        for k in range(len(beside)):
            turn_copy(w, k).start()
        pass_on(w, near, 0)

    def settle(w):
        arrive(w, diagonal)
        pass_on(w, diagonal, len(near))
        own_weight(w).wait()
        arrive(w, (partner, *partner_core))

    turn(0)
    for w in range(2, len(weights)):
        send(w)
    turn(1)
    settle(0)
    query_ref[...] = silu(
        jnp.dot(
            items_ref[...], candidate_weight_ref[:, :width], preferred_element_type=jnp.float32
        )
    ).astype(jnp.bfloat16)
    gate_ref[...] = (
        silu(
            jnp.dot(
                items_ref[...], candidate_weight_ref[:, width:], preferred_element_type=jnp.float32
            )
        )
        * gain_ref[...]
    )
    relay(0)
    settle(1)
    for w in range(2, len(weights)):
        turn(w)
    for i in range(1, ahead):
        relay(i)
    for w in range(2, len(weights)):
        settle(w)
    for i in range(max(1, ahead), lead):
        relay(i)

    @pl.loop(0, requests)
    def _(i):
        @pl.when((i >= lead - ahead) & (i + ahead < requests))
        def _():
            relay(i + ahead)

        own_event(i).wait()
        for k, source in enumerate(others):

            @pl.when(jnp.logical_not(is_relayed(source)))
            def _():
                event_copy(i, k, source, source).wait_recv()

        length = length_ref[i]
        inverse = 1.0 / jnp.full((1, 1), length, jnp.int32).astype(jnp.float32)
        pairs_ref[:, :width] = silu(
            jnp.dot(
                events_ref[i], history_weight_ref[:, :width], preferred_element_type=jnp.float32
            )
        ).astype(jnp.bfloat16)
        live = lax.broadcasted_iota(jnp.int32, (history_total, width), 0) < length
        pairs_ref[:, width:] = jnp.where(
            live,
            silu(
                jnp.dot(
                    events_ref[i], history_weight_ref[:, width:], preferred_element_type=jnp.float32
                )
            ),
            0.0,
        ).astype(jnp.bfloat16)
        for h in range(HEADS):
            part = slice(h * head, (h + 1) * head)
            scores = half_scale * lax.dot_general(
                query_ref[:, part],
                pairs_ref[:, part],
                (((1,), (1,)), ((), ())),
                preferred_element_type=jnp.float32,
            )
            mixed = ((scores + scores * jnp.tanh(scores)) * inverse).astype(jnp.bfloat16)
            attended_ref[:, part] = jnp.dot(
                mixed,
                pairs_ref[:, width + h * head : width + (h + 1) * head],
                preferred_element_type=jnp.float32,
            )

        @pl.when(i > 0)
        def _():
            for k, target in enumerate(others):
                logit_copy(i - 1, k, target, shard).start()

        attended = attended_ref[...]
        center = attended - jnp.mean(attended, axis=-1, keepdims=True)
        spread = jnp.mean(center * center, axis=-1, keepdims=True)
        normed = (center * lax.rsqrt(spread + EPSILON) * gate_ref[...]).astype(jnp.bfloat16)
        merged = (
            jnp.dot(normed, output_weight_ref[...], preferred_element_type=jnp.float32)
            + items_ref[...].astype(jnp.float32)
        ).astype(jnp.bfloat16)
        hidden = silu(
            jnp.dot(merged, hidden_weight_ref[...], preferred_element_type=jnp.float32)
        ).astype(jnp.bfloat16)
        logits_ref[shard, i] = lax.dot_general(
            score_weight_ref[...],
            hidden,
            (((1,), (1,)), ((), ())),
            preferred_element_type=jnp.float32,
        )

    for w in range(len(weights)):
        for k, target in enumerate((*near, partner)):
            weight_copy(w, target, group, weight_send.at[w, k]).wait_send()
        for k, source in enumerate(same_core):
            pass_copy(w, k, source).wait_send()
        for k in range(len(beside)):
            turn_copy(w, k).wait_send()

    @pl.loop(0, requests)
    def _(i):
        for k, target in enumerate(others):

            @pl.when(jnp.logical_not(is_far(target)))
            def _():
                event_copy(i, k, target, shard).wait_send()

        for k, (middle, _, _) in enumerate(relays):

            @pl.when(shard == middle)
            def _():
                relay_copy(i, k).wait_send()

    for k, target in enumerate(others):
        logit_copy(requests - 1, k, target, shard).start()

    @pl.loop(0, requests)
    def _(i):
        for k, target in enumerate(others):
            logit_copy(i, k, target, shard).wait_send()
            logit_copy(i, k, target, target).wait_recv()


def pair_logits(
    history, length, items, history_weight, candidate_weight, output_weight, hidden_weight, gain,
    score_weight,
):
    requests, own_events, width = history.shape
    rows = items.shape[0]
    groups, shards = lax.axis_size("req"), lax.axis_size("cand")
    history_total = own_events * shards
    whole = pl.BlockSpec(memory_space=pltpu.VMEM)
    apart = pl.BlockSpec(memory_space=pl.ANY)
    weights = (history_weight, candidate_weight, output_weight, hidden_weight)
    count = len(weights)
    return pl.pallas_call(
        functools.partial(pair_kernel, groups, shards),
        out_shape=jax.ShapeDtypeStruct((shards, requests, score_weight.shape[0], rows), jnp.float32),
        in_specs=[
            pl.BlockSpec(memory_space=pltpu.SMEM),
            apart, whole, apart, apart, apart, apart, whole, whole,
        ],
        out_specs=whole,
        scratch_shapes=[
            pltpu.VMEM((requests, history_total, width), jnp.bfloat16),
            *(
                pltpu.VMEM((weight.shape[0] * groups, weight.shape[1]), jnp.bfloat16)
                for weight in weights
            ),
            pltpu.VMEM((rows, width), jnp.bfloat16),
            pltpu.VMEM((rows, width), jnp.float32),
            pltpu.VMEM((history_total, 2 * width), jnp.bfloat16),
            pltpu.VMEM((rows, width), jnp.float32),
            pltpu.SemaphoreType.DMA((count, groups // 2)),
            pltpu.SemaphoreType.DMA((count, groups)),
            pltpu.SemaphoreType.DMA((count, groups // 2)),
            pltpu.SemaphoreType.DMA((count, groups // 2)),
            pltpu.SemaphoreType.DMA((requests, shards + 1)),
            pltpu.SemaphoreType.DMA((requests, shards)),
            pltpu.SemaphoreType.DMA((requests, shards)),
            pltpu.SemaphoreType.DMA((requests, shards)),
            pltpu.SemaphoreType.DMA((count + requests,)),
        ],
        compiler_params=pltpu.CompilerParams(
            collective_id=0, has_side_effects=True, vmem_limit_bytes=58 * 1024 * 1024
        ),
    )(
        length, history, items, history_weight, candidate_weight, output_weight, hidden_weight,
        gain, score_weight,
    )


def blend(logits, candidate_count, block_shard, block_index, item_ages, item_blocks):
    shards = lax.axis_size("cand")
    mine = lax.axis_index("cand")
    requests, max_blocks = block_shard.shape
    per_scorer = max_blocks // shards
    logits = logits.reshape(shards, requests, -1, item_blocks, BLOCK)
    ids = lax.dynamic_slice_in_dim(
        block_shard * item_blocks + block_index, mine * per_scorer, per_scorer, 1
    )
    names = jnp.arange(shards * item_blocks, dtype=jnp.int32).reshape(shards, 1, 1, item_blocks, 1)
    picked = ids[None, :, :, None, None] == names
    first, second = (
        jnp.sum(jnp.where(picked, logits[:, :, None, c], 0.0), axis=(0, 3)) for c in (0, 1)
    )
    decays = jnp.exp(
        -item_ages.astype(jnp.float32).reshape(requests, per_scorer, BLOCK) / AGE_SCALE
    )
    blended = decays * first + (1.0 - decays) * second
    row_number = (mine * per_scorer + jnp.arange(per_scorer, dtype=jnp.int32))[
        None, :, None
    ] * BLOCK + jnp.arange(BLOCK, dtype=jnp.int32)[None, None, :]
    kept_rows = row_number < candidate_count[:, None, None]
    return jnp.where(kept_rows, blended, 0.0).reshape(requests, per_scorer * BLOCK)


def local(
    history,
    history_length,
    candidate_count,
    block_shard,
    block_index,
    item_table,
    item_ages,
    history_weight,
    candidate_weight,
    output_weight,
    hidden_weight,
    norm_gain,
    score_weight,
):
    item_blocks = item_table.shape[0]
    logits = pair_logits(
        history,
        history_length,
        item_table.reshape(-1, item_table.shape[2]),
        history_weight,
        candidate_weight,
        output_weight,
        hidden_weight,
        norm_gain[None, :],
        score_weight,
    )
    return blend(logits, candidate_count, block_shard, block_index, item_ages, item_blocks)


def solution(mesh):
    return jax.shard_map(
        local,
        mesh=mesh,
        in_specs=(
            P("req", "cand", None),
            P("req"),
            P("req"),
            P("req", None),
            P("req", None),
            P("cand", None, None),
            P("req", "cand"),
            P("req", None),
            P("req", None),
            P("req", None),
            P("req", None),
            P(),
            P(),
        ),
        out_specs=P("req", "cand"),
        check_vma=False,
    )
```

profile of v0, /device:TPU:0, one launch (start us, length us, event | category | flops | bytes accessed | tf_op | source)
XLA Modules:
  0.0 109.0 jit_solution(2224930957571086352)
XLA Ops:
  0.0 105.4 %shard_map.127 = f32[4,8,2,512]{3,2,1,0:T(2,128)} custom-call(s32[8]{0:T(128)} %length_ref.1, bf16[8,64,1024]{2,1,0:T(8,128)(2,1)} %history_ref.1, bf16[512,1024]{1,0:T(8,128)(2,1)} %bitcast.21, bf16[128,2048]{1,0:T(8,128)(2,1)} %history_shard_ref.1, bf16[128,2048]{1,0:T(8,128)(2,1)} %candidate_shard_ref.1, bf16[128,1024]{1,0:T(8,128)(2,1)} %output_shard_ref.1, ...), custom_call_target="tpu_custom_call" | custom-call | tf_op jit(solution)/shard_map/pallas_call | solution.py:369
  105.4 1.0 reshape.75
  106.4 0.0 copy-start.1
  106.5 0.0 copy-start.2
  106.5 0.6 copy-done.1
  107.1 0.0 copy-done.2
  107.2 0.1 constant_dynamic-slice_fusion
  107.2 0.1 broadcast_compare_fusion
  107.3 0.0 copy-start
  107.3 0.2 select_reduce_fusion.1
  107.6 0.1 add.56
  107.6 0.0 copy-start.3
  107.6 0.4 copy-done
  108.1 0.2 copy-done.3
  108.3 0.7 fusion.1
  (5 shorter events, 0.0 us)
Async XLA Ops:
  106.4 0.7 copy-start.1
  106.5 0.7 copy-start.2
  107.3 0.8 copy-start
  107.6 0.7 copy-start.3
where the time goes:
time: 109 us
  Pallas kernels  105 us (96%)
  local copies, waits for them, and re-layouts  2.51 us (2%)
    pallas_call x1, Pallas kernels, pair_logits(): pl.pallas_call(functools.partial(pair_kernel, groups, shards), out_shape=...  105 us

commit v1 on v0

v1 whole, which is shorter than its diff:
```python
import functools
import math

import jax
import jax.numpy as jnp
from jax import lax
from jax.experimental import pallas as pl
from jax.experimental.pallas import tpu as pltpu
from jax.sharding import PartitionSpec as P

HEADS = 8
BLOCK = 128
EPSILON = 1e-05
AGE_SCALE = 48.0
PARTS = 2


def silu(value):
    half = 0.5 * value
    return half + half * jnp.tanh(half)


MESH = pl.DeviceIdType.MESH


def pair_kernel(
    groups,
    shards,
    length_ref,
    history_ref,
    item_shard_ref,
    history_shard_ref,
    candidate_shard_ref,
    output_shard_ref,
    hidden_shard_ref,
    gain_ref,
    score_weight_ref,
    logits_ref,
    events_ref,
    items_ref,
    query_weight_ref,
    key_weight_ref,
    value_weight_ref,
    gate_weight_ref,
    output_weight_ref,
    hidden_weight_ref,
    query_ref,
    gate_ref,
    pairs_ref,
    attended_ref,
    weight_send,
    weight_recv,
    pass_send,
    turn_send,
    cross_send,
    cross_recv,
    event_send,
    event_recv,
    logit_send,
    logit_recv,
    own_sem,
    own_event_sem,
):
    group = lax.axis_index("req")
    shard = lax.axis_index("cand")
    partner = group + 1 - 2 * lax.rem(group, 2)
    own_events = history_ref.shape[1]
    width = history_ref.shape[2]
    lanes = shards // PARTS
    part, lane = lax.div(shard, lanes), lax.rem(shard, lanes)
    mate = lax.rem(shard + lanes, shards)
    requests, history_total = events_ref.shape[:2]
    chunks, _, span = query_weight_ref.shape
    batches = requests // chunks
    rows = item_shard_ref.shape[0]
    head = width // HEADS
    half_scale = 0.5 / math.sqrt(head)
    depth = history_shard_ref.shape[0]
    item_depth = rows // groups
    half = groups // 2
    row, core = lax.div(group, half), lax.rem(group, 2)
    across = lax.rem(group + half, groups)
    beside = [row * half + lax.rem(group - row * half + 2 * d, half) for d in range(1, half // 2)]
    diagonal = [lax.rem(source + half, groups) for source in beside]
    near = (*beside, across)
    same_core = (*near, *diagonal)
    partner_core = [source + partner - group for source in same_core]
    others = [lax.rem(shard + d, shards) for d in range(1, shards)]
    relays = ((1, 2, 0), (2, 1, 3)) if shards == 4 else ()

    def rows_of(source):
        return pl.ds(pl.multiple_of(source * depth, depth), depth)

    def item_rows(source):
        return pl.ds(pl.multiple_of(source * item_depth, item_depth), item_depth)

    def events_of(source):
        return pl.ds(pl.multiple_of(source * own_events, own_events), own_events)

    def columns(start):
        return pl.ds(pl.multiple_of(start, span), span)

    item_piece = (
        0,
        items_ref.at[1 - part, item_rows(group)],
        lambda source: items_ref.at[1 - part, item_rows(source)],
    )

    def chunk_pieces(c):
        return (
            (
                1 + 3 * c,
                candidate_shard_ref.at[:, columns(c * span)],
                lambda source: query_weight_ref.at[c, rows_of(source)],
            ),
            (
                2 + 3 * c,
                history_shard_ref.at[:, columns(c * span)],
                lambda source: key_weight_ref.at[c, rows_of(source)],
            ),
            (
                3 + 3 * c,
                history_shard_ref.at[:, columns(width + c * span)],
                lambda source: value_weight_ref.at[c, rows_of(source)],
            ),
        )

    gate_piece = (
        1 + 3 * chunks,
        candidate_shard_ref.at[:, width:],
        lambda source: gate_weight_ref.at[rows_of(source)],
    )
    output_piece = (
        2 + 3 * chunks,
        output_shard_ref,
        lambda source: output_weight_ref.at[rows_of(source)],
    )
    hidden_piece = (
        3 + 3 * chunks,
        hidden_shard_ref,
        lambda source: hidden_weight_ref.at[rows_of(source)],
    )

    def weight_copy(piece, k, target, source):
        w, own, place = piece
        return pltpu.make_async_remote_copy(
            src_ref=own,
            dst_ref=place(source),
            send_sem=weight_send.at[w, k],
            recv_sem=weight_recv.at[w, source],
            device_id={"req": target},
            device_id_type=MESH,
        )

    def pass_copy(piece, k, source):
        w, _, place = piece
        return pltpu.make_async_remote_copy(
            src_ref=place(source),
            dst_ref=place(source),
            send_sem=pass_send.at[w, k],
            recv_sem=weight_recv.at[w, source],
            device_id={"req": partner},
            device_id_type=MESH,
        )

    def turn_copy(piece, k):
        w, _, place = piece
        source = beside[k] + core * (across - beside[k])
        target = across + core * (beside[k] - across)
        return pltpu.make_async_remote_copy(
            src_ref=place(source),
            dst_ref=place(source),
            send_sem=turn_send.at[w, k],
            recv_sem=weight_recv.at[w, source],
            device_id={"req": target},
            device_id_type=MESH,
        )

    def own_piece(piece):
        w, own, place = piece
        return pltpu.make_async_copy(own, place(group), own_sem.at[w])

    def send(pieces):
        for piece in pieces:
            for k, target in enumerate((*near, partner)):
                weight_copy(piece, k, target, group).start()

    def arrive(piece, sources):
        for source in sources:
            weight_copy(piece, 0, partner, source).wait_recv()

    def turn(pieces):
        for piece in pieces:
            arrive(piece, near)
            for k in range(len(beside)):
                turn_copy(piece, k).start()
            for k, source in enumerate(near):
                pass_copy(piece, k, source).start()

    def settle(pieces):
        for piece in pieces:
            arrive(piece, diagonal)
            for k, source in enumerate(diagonal):
                pass_copy(piece, len(near) + k, source).start()
        for piece in pieces:
            arrive(piece, (partner, *partner_core))

    def finish(pieces):
        for piece in pieces:
            for k, target in enumerate((*near, partner)):
                weight_copy(piece, k, target, group).wait_send()
            for k, source in enumerate(same_core):
                pass_copy(piece, k, source).wait_send()
            for k in range(len(beside)):
                turn_copy(piece, k).wait_send()

    def cross_copy():
        return pltpu.make_async_remote_copy(
            src_ref=item_shard_ref.at[item_rows(group)],
            dst_ref=items_ref.at[part, item_rows(group)],
            send_sem=cross_send,
            recv_sem=cross_recv,
            device_id={"cand": mate},
            device_id_type=MESH,
        )

    def cross_arrival():
        return pltpu.make_async_remote_copy(
            src_ref=item_shard_ref.at[item_rows(group)],
            dst_ref=items_ref.at[1 - part, item_rows(group)],
            send_sem=cross_send,
            recv_sem=cross_recv,
            device_id={"cand": mate},
            device_id_type=MESH,
        )

    def own_items():
        return pltpu.make_async_copy(item_shard_ref, items_ref.at[part], own_sem.at[0])

    def event_copy(i, k, target, source):
        return pltpu.make_async_remote_copy(
            src_ref=history_ref.at[lax.div(target, lanes) * requests + i],
            dst_ref=events_ref.at[i, events_of(source)],
            send_sem=event_send.at[i, k],
            recv_sem=event_recv.at[i, source],
            device_id={"cand": target},
            device_id_type=MESH,
        )

    def relay_copy(i, k):
        _, source, target = relays[k]
        return pltpu.make_async_remote_copy(
            src_ref=events_ref.at[i, events_of(source)],
            dst_ref=events_ref.at[i, events_of(source)],
            send_sem=event_send.at[i, len(others) + k],
            recv_sem=event_recv.at[i, source],
            device_id={"cand": target},
            device_id_type=MESH,
        )

    def direct(target):
        flag = shard >= 0
        for _, source, end in relays:
            flag = flag & ((shard != source) | (target != end))
        return flag

    def own_event(i):
        return pltpu.make_async_copy(
            history_ref.at[part * requests + i],
            events_ref.at[i, events_of(shard)],
            own_event_sem.at[i],
        )

    def logit_copy(i, k, target, source):
        place = logits_ref.at[lax.rem(source, lanes), lax.div(source, lanes) * requests + i]
        return pltpu.make_async_remote_copy(
            src_ref=place,
            dst_ref=place,
            send_sem=logit_send.at[i, k],
            recv_sem=logit_recv.at[i, source],
            device_id={"cand": target},
            device_id_type=MESH,
        )

    own_items().start()
    for c in range(chunks):
        for piece in chunk_pieces(c):
            own_piece(piece).start()
    for piece in (gate_piece, output_piece, hidden_piece):
        own_piece(piece).start()

    barrier = pltpu.get_barrier_semaphore()
    for target in (*near, partner):
        pl.semaphore_signal(barrier, inc=1, device_id={"req": target}, device_id_type=MESH)
    for target in others:
        pl.semaphore_signal(barrier, inc=1, device_id={"cand": target}, device_id_type=MESH)
    pl.semaphore_wait(barrier, len(near) + 1 + len(others))

    cross_copy().start()
    send(chunk_pieces(0))

    @pl.loop(0, requests)
    def _(i):
        for k, target in enumerate(others):

            @pl.when(direct(target))
            def _():
                event_copy(i, k, target, shard).start()

        own_event(i).start()

    send(chunk_pieces(1))
    cross_arrival().wait_recv()
    send((item_piece,))
    turn(chunk_pieces(0))
    if chunks > 2:
        send(chunk_pieces(2))
    turn((item_piece,))
    own_items().wait()
    settle((item_piece,))
    for c in range(chunks):
        for piece in chunk_pieces(c):
            own_piece(piece).wait()
    for piece in (gate_piece, output_piece, hidden_piece):
        own_piece(piece).wait()

    def enter_chunk(d):
        @pl.when(d + 1 < chunks)
        def _():
            turn(chunk_pieces(d + 1))

        @pl.when(d + 3 < chunks)
        def _():
            send(chunk_pieces(d + 3))

        @pl.when(d + 3 == chunks)
        def _():
            send((gate_piece,))

        @pl.when(d + 2 == chunks)
        def _():
            send((output_piece, hidden_piece))

        @pl.when(d + 1 == chunks)
        def _():
            turn((gate_piece,))

        settle(chunk_pieces(d))
        query_ref[d] = (
            half_scale
            * silu(
                jnp.dot(
                    items_ref[...].reshape(PARTS * rows, width),
                    query_weight_ref[d],
                    preferred_element_type=jnp.float32,
                )
            )
        ).astype(jnp.bfloat16)

    def enter_request(i):
        own_event(i).wait()
        for source in others:
            event_copy(i, 0, mate, source).wait_recv()
        for k, (middle, _, _) in enumerate(relays):

            @pl.when(shard == middle)
            def _():
                relay_copy(i, k).start()

    def attend(c, r, i):
        length = length_ref[part * requests + i]
        events = events_ref[i]
        pairs_ref[0] = silu(
            jnp.dot(events, key_weight_ref[c], preferred_element_type=jnp.float32)
        ).astype(jnp.bfloat16)
        live = lax.broadcasted_iota(jnp.int32, (history_total, span), 0) < length
        pairs_ref[1] = jnp.where(
            live,
            silu(jnp.dot(events, value_weight_ref[c], preferred_element_type=jnp.float32)),
            0.0,
        ).astype(jnp.bfloat16)
        for h in range(span // head):
            lanes_of = slice(h * head, (h + 1) * head)
            scores = lax.dot_general(
                query_ref[c, :, lanes_of],
                pairs_ref[0, :, lanes_of],
                (((1,), (1,)), ((), ())),
                preferred_element_type=jnp.float32,
            )
            mixed = (scores + scores * jnp.tanh(scores)).astype(jnp.bfloat16)
            attended_ref[r, c, :, lanes_of] = jnp.dot(
                mixed, pairs_ref[1, :, lanes_of], preferred_element_type=jnp.float32
            )

    def run_batch(b):
        @pl.loop(0, chunks * chunks)
        def _(t):
            d = t * 0
            for edge in range(1, chunks):
                d = d + (t >= edge * edge).astype(jnp.int32)
            k = t - d * d
            c = jnp.where(k < d, d, k - d)
            r = jnp.where(k < d, k, d)
            i = b * chunks + r

            @pl.when((k == 0) & (b == 0))
            def _():
                enter_chunk(d)

            @pl.when(k == d)
            def _():
                enter_request(i)

            attend(c, r, i)

        @pl.when(b == 0)
        def _():
            turn((output_piece, hidden_piece))
            settle((gate_piece,))
            gate_ref[...] = (
                silu(
                    jnp.dot(
                        items_ref[...].reshape(PARTS * rows, width),
                        gate_weight_ref[...],
                        preferred_element_type=jnp.float32,
                    )
                )
                * gain_ref[...]
            )
            settle((output_piece, hidden_piece))

        @pl.loop(0, chunks)
        def _(r):
            i = b * chunks + r
            length = jnp.full((1, 1), length_ref[part * requests + i], jnp.int32).astype(
                jnp.float32
            )

            @pl.loop(0, PARTS)
            def _(p):
                tile = pl.ds(pl.multiple_of(p * rows, rows), rows)
                attended = jnp.concatenate(
                    [attended_ref[r, c, tile] for c in range(chunks)], axis=-1
                )
                center = attended - jnp.mean(attended, axis=-1, keepdims=True)
                spread = jnp.mean(center * center, axis=-1, keepdims=True)
                normed = (
                    center * lax.rsqrt(spread + EPSILON * length * length) * gate_ref[tile]
                ).astype(jnp.bfloat16)
                merged = (
                    jnp.dot(normed, output_weight_ref[...], preferred_element_type=jnp.float32)
                    + items_ref[p].astype(jnp.float32)
                ).astype(jnp.bfloat16)
                hidden = silu(
                    jnp.dot(merged, hidden_weight_ref[...], preferred_element_type=jnp.float32)
                ).astype(jnp.bfloat16)
                logits_ref[lane, part * requests + i, p] = lax.dot_general(
                    score_weight_ref[...],
                    hidden,
                    (((1,), (1,)), ((), ())),
                    preferred_element_type=jnp.float32,
                )

            for k, target in enumerate(others):
                logit_copy(i, k, target, shard).start()

    if batches == 1:
        run_batch(0)
    else:

        @pl.loop(0, batches)
        def _(b):
            run_batch(b)

    cross_copy().wait_send()
    finish((item_piece, gate_piece, output_piece, hidden_piece))

    @pl.loop(0, chunks)
    def _(c):
        finish(chunk_pieces(c))

    @pl.loop(0, requests)
    def _(i):
        for k, target in enumerate(others):

            @pl.when(direct(target))
            def _():
                event_copy(i, k, target, shard).wait_send()

        for k, (middle, _, _) in enumerate(relays):

            @pl.when(shard == middle)
            def _():
                relay_copy(i, k).wait_send()

        for k, target in enumerate(others):
            logit_copy(i, k, target, shard).wait_send()
            logit_copy(i, k, target, target).wait_recv()


def pair_logits(
    history, length, items, history_weight, candidate_weight, output_weight, hidden_weight, gain,
    score_weight,
):
    all_requests, own_events, width = history.shape
    rows = items.shape[0]
    groups, shards = lax.axis_size("req"), lax.axis_size("cand")
    history_total = own_events * shards
    requests = all_requests // PARTS
    chunks = HEADS // 2
    span = width // chunks
    depth = history_weight.shape[0] * groups
    pieces = 4 + 3 * chunks
    whole = pl.BlockSpec(memory_space=pltpu.VMEM)
    apart = pl.BlockSpec(memory_space=pl.ANY)
    return pl.pallas_call(
        functools.partial(pair_kernel, groups, shards),
        out_shape=jax.ShapeDtypeStruct(
            (shards // PARTS, all_requests, PARTS, score_weight.shape[0], rows), jnp.float32
        ),
        in_specs=[
            pl.BlockSpec(memory_space=pltpu.SMEM),
            apart, apart, apart, apart, apart, apart, whole, whole,
        ],
        out_specs=whole,
        scratch_shapes=[
            pltpu.VMEM((requests, history_total, width), jnp.bfloat16),
            pltpu.VMEM((PARTS, rows, width), jnp.bfloat16),
            pltpu.VMEM((chunks, depth, span), jnp.bfloat16),
            pltpu.VMEM((chunks, depth, span), jnp.bfloat16),
            pltpu.VMEM((chunks, depth, span), jnp.bfloat16),
            pltpu.VMEM((depth, width), jnp.bfloat16),
            pltpu.VMEM((depth, width), jnp.bfloat16),
            pltpu.VMEM((depth, hidden_weight.shape[1]), jnp.bfloat16),
            pltpu.VMEM((chunks, PARTS * rows, span), jnp.bfloat16),
            pltpu.VMEM((PARTS * rows, width), jnp.float32),
            pltpu.VMEM((2, history_total, span), jnp.bfloat16),
            pltpu.VMEM((chunks, chunks, PARTS * rows, span), jnp.float32),
            pltpu.SemaphoreType.DMA((pieces, groups // 2)),
            pltpu.SemaphoreType.DMA((pieces, groups)),
            pltpu.SemaphoreType.DMA((pieces, groups // 2)),
            pltpu.SemaphoreType.DMA((pieces, groups // 2)),
            pltpu.SemaphoreType.DMA,
            pltpu.SemaphoreType.DMA,
            pltpu.SemaphoreType.DMA((requests, shards + 1)),
            pltpu.SemaphoreType.DMA((requests, shards)),
            pltpu.SemaphoreType.DMA((requests, shards)),
            pltpu.SemaphoreType.DMA((requests, shards)),
            pltpu.SemaphoreType.DMA((pieces,)),
            pltpu.SemaphoreType.DMA((requests,)),
        ],
        compiler_params=pltpu.CompilerParams(
            collective_id=0, has_side_effects=True, vmem_limit_bytes=60 * 1024 * 1024
        ),
    )(
        length, history, items, history_weight, candidate_weight, output_weight, hidden_weight,
        gain, score_weight,
    )


def blend(logits, candidate_count, block_shard, block_index, item_ages, item_blocks):
    shards = lax.axis_size("cand")
    mine = lax.axis_index("cand")
    lanes = shards // PARTS
    requests, max_blocks = block_shard.shape
    per_scorer = max_blocks // shards
    logits = logits.reshape(lanes, requests, PARTS, -1, item_blocks, BLOCK)
    ids = lax.dynamic_slice_in_dim(
        block_shard * item_blocks + block_index, mine * per_scorer, per_scorer, 1
    )
    names = (
        jnp.arange(shards * item_blocks, dtype=jnp.int32)
        .reshape(PARTS, lanes, item_blocks)
        .transpose(1, 0, 2)[:, None, :, None, :, None]
    )
    picked = ids[None, :, None, :, None, None] == names
    first, second = (
        jnp.sum(jnp.where(picked, logits[:, :, :, None, c], 0.0), axis=(0, 2, 4)) for c in (0, 1)
    )
    decays = jnp.exp(
        -item_ages.astype(jnp.float32).reshape(requests, per_scorer, BLOCK) / AGE_SCALE
    )
    blended = decays * first + (1.0 - decays) * second
    row_number = (mine * per_scorer + jnp.arange(per_scorer, dtype=jnp.int32))[
        None, :, None
    ] * BLOCK + jnp.arange(BLOCK, dtype=jnp.int32)[None, None, :]
    kept_rows = row_number < candidate_count[:, None, None]
    return jnp.where(kept_rows, blended, 0.0).reshape(requests, per_scorer * BLOCK)


def local(
    history,
    history_length,
    candidate_count,
    block_shard,
    block_index,
    item_table,
    item_ages,
    history_weight,
    candidate_weight,
    output_weight,
    hidden_weight,
    norm_gain,
    score_weight,
):
    item_blocks = item_table.shape[0]
    logits = pair_logits(
        history,
        history_length,
        item_table.reshape(-1, item_table.shape[2]),
        history_weight,
        candidate_weight,
        output_weight,
        hidden_weight,
        norm_gain[None, :],
        score_weight,
    )
    return blend(logits, candidate_count, block_shard, block_index, item_ages, item_blocks)


def solution(mesh):
    return jax.shard_map(
        local,
        mesh=mesh,
        in_specs=(
            P("req", "cand", None),
            P("req"),
            P("req"),
            P("req", None),
            P("req", None),
            P("cand", None, None),
            P("req", "cand"),
            P("req", None),
            P("req", None),
            P("req", None),
            P("req", None),
            P(),
            P(),
        ),
        out_specs=P("req", "cand"),
        check_vma=False,
    )
```

time: 109 us -> 102 us (0.936)
  Pallas kernels: 105 us -> 98.5 us
    pallas_call x1, Pallas kernels: 105 us -> 98.5 us  [pair_logits(): pl.pallas_call(functools.partial(pair_kernel, groups, shards), out_shape=...]
where the time goes in v1:
time: 102 us
  Pallas kernels  98.5 us (97%)
  local copies, waits for them, and re-layouts  2.51 us (2%)
    pallas_call x1, Pallas kernels, pair_logits(): pl.pallas_call(functools.partial(pair_kernel, groups, shards), out_shape=...  98.5 us

profile of v1, /device:TPU:0, one launch (start us, length us, event | category | flops | bytes accessed | tf_op | source)
XLA Modules:
  0.0 102.1 jit_solution(12183429181563878919)
XLA Ops:
  0.0 98.5 %shard_map.127 = f32[2,8,2,2,512]{4,3,2,1,0:T(2,128)} custom-call(s32[8]{0:T(128)} %length_ref.1, bf16[8,64,1024]{2,1,0:T(8,128)(2,1)} %history_ref.1, bf16[512,1024]{1,0:T(8,128)(2,1)} %bitcast.21, bf16[128,2048]{1,0:T(8,128)(2,1)} %history_shard_ref.1, bf16[128,2048]{1,0:T(8,128)(2,1)} %candidate_shard_ref.1, bf16[128,1024]{1,0:T(8,128)(2,1)} %output_shard_ref.1, ...), custom_call_target="tpu_custom_call" | custom-call | tf_op jit(solution)/shard_map/pallas_call | solution.py:516
  98.5 1.0 %reshape.81 = f32[2,8,2,2,4,128]{5,4,3,2,1,0:T(4,128)S(1)} reshape(f32[2,8,2,2,512]{4,3,2,1,0:T(2,128)} %shard_map.127) | data formatting | bytes 262144 | tf_op jit(solution)/shard_map/reshape | solution.py:567
  99.6 0.0 copy-start.1
  99.6 0.0 copy-start.2
  99.6 0.6 copy-done.1
  100.3 0.0 copy-done.2
  100.3 0.1 constant_dynamic-slice_fusion
  100.3 0.1 broadcast_compare_fusion
  100.4 0.0 copy-start
  100.5 0.2 select_reduce_fusion.1
  100.7 0.1 add.56
  100.8 0.0 copy-start.3
  100.8 0.4 copy-done
  101.2 0.2 copy-done.3
  101.4 0.7 fusion.1
  (5 shorter events, 0.0 us)
Async XLA Ops:
  99.6 0.7 copy-start.1
  99.6 0.7 copy-start.2
  100.4 0.8 copy-start
  100.8 0.7 copy-start.3

commit v2 on v1

--- a/solution.py
+++ b/solution.py
@@ -48,6 +48,7 @@
     gate_ref,
     pairs_ref,
     attended_ref,
+    normed_ref,
     weight_send,
     weight_recv,
     pass_send,
@@ -296,55 +297,52 @@
         pl.semaphore_signal(barrier, inc=1, device_id={"cand": target}, device_id_type=MESH)
     pl.semaphore_wait(barrier, len(near) + 1 + len(others))
 
+    late = {chunks: (gate_piece,), chunks + 1: (output_piece, hidden_piece)}
+
+    def at_level(action, level):
+        @pl.when(level < chunks)
+        def _():
+            action(chunk_pieces(level))
+
+        for edge, pieces in late.items():
+
+            @pl.when(level == edge)
+            def _():
+                action(pieces)
+
+    def send_events(i):
+        for k, target in enumerate(others):
+
+            @pl.when(direct(target))
+            def _():
+                event_copy(i, k, target, shard).start()
+
+        own_event(i).start()
+
+    send(chunk_pieces(0))
     cross_copy().start()
-    send(chunk_pieces(0))
+    send(chunk_pieces(1))
 
     @pl.loop(0, requests)
     def _(i):
-        for k, target in enumerate(others):
-
-            @pl.when(direct(target))
-            def _():
-                event_copy(i, k, target, shard).start()
-
-        own_event(i).start()
-
-    send(chunk_pieces(1))
+        send_events(i)
+
+    turn(chunk_pieces(0))
+    at_level(send, 2)
     cross_arrival().wait_recv()
     send((item_piece,))
-    turn(chunk_pieces(0))
-    if chunks > 2:
-        send(chunk_pieces(2))
-    turn((item_piece,))
+    turn(chunk_pieces(1))
     own_items().wait()
-    settle((item_piece,))
     for c in range(chunks):
         for piece in chunk_pieces(c):
             own_piece(piece).wait()
     for piece in (gate_piece, output_piece, hidden_piece):
         own_piece(piece).wait()
+    turn((item_piece,))
+    settle((item_piece,))
 
     def enter_chunk(d):
-        @pl.when(d + 1 < chunks)
-        def _():
-            turn(chunk_pieces(d + 1))
-
-        @pl.when(d + 3 < chunks)
-        def _():
-            send(chunk_pieces(d + 3))
-
-        @pl.when(d + 3 == chunks)
-        def _():
-            send((gate_piece,))
-
-        @pl.when(d + 2 == chunks)
-        def _():
-            send((output_piece, hidden_piece))
-
-        @pl.when(d + 1 == chunks)
-        def _():
-            turn((gate_piece,))
-
+        at_level(send, d + 3)
         settle(chunk_pieces(d))
         query_ref[d] = (
             half_scale
@@ -357,15 +355,27 @@
             )
         ).astype(jnp.bfloat16)
 
+    def relay(i):
+        for k, (middle, source, _) in enumerate(relays):
+
+            @pl.when(shard == middle)
+            def _():
+                event_copy(i, 0, mate, source).wait_recv()
+                relay_copy(i, k).start()
+
+    def relayed(source):
+        flag = shard < 0
+        for middle, start, _ in relays:
+            flag = flag | ((shard == middle) & (source == start))
+        return flag
+
     def enter_request(i):
         own_event(i).wait()
         for source in others:
-            event_copy(i, 0, mate, source).wait_recv()
-        for k, (middle, _, _) in enumerate(relays):
-
-            @pl.when(shard == middle)
-            def _():
-                relay_copy(i, k).start()
+
+            @pl.when(jnp.logical_not(relayed(source)))
+            def _():
+                event_copy(i, 0, mate, source).wait_recv()
 
     def attend(c, r, i):
         length = length_ref[part * requests + i]
@@ -403,9 +413,17 @@
             r = jnp.where(k < d, k, d)
             i = b * chunks + r
 
+            @pl.when(k == 0)
+            def _():
+                relay(b * chunks + d)
+
             @pl.when((k == 0) & (b == 0))
             def _():
                 enter_chunk(d)
+
+            @pl.when((k == d) & (b == 0))
+            def _():
+                at_level(turn, d + 2)
 
             @pl.when(k == d)
             def _():
@@ -415,7 +433,6 @@
 
         @pl.when(b == 0)
         def _():
-            turn((output_piece, hidden_piece))
             settle((gate_piece,))
             gate_ref[...] = (
                 silu(
@@ -427,14 +444,12 @@
                 )
                 * gain_ref[...]
             )
-            settle((output_piece, hidden_piece))
 
         @pl.loop(0, chunks)
         def _(r):
-            i = b * chunks + r
-            length = jnp.full((1, 1), length_ref[part * requests + i], jnp.int32).astype(
-                jnp.float32
-            )
+            length = jnp.full(
+                (1, 1), length_ref[part * requests + b * chunks + r], jnp.int32
+            ).astype(jnp.float32)
 
             @pl.loop(0, PARTS)
             def _(p):
@@ -444,22 +459,32 @@
                 )
                 center = attended - jnp.mean(attended, axis=-1, keepdims=True)
                 spread = jnp.mean(center * center, axis=-1, keepdims=True)
-                normed = (
+                normed_ref[r, tile] = (
                     center * lax.rsqrt(spread + EPSILON * length * length) * gate_ref[tile]
                 ).astype(jnp.bfloat16)
-                merged = (
-                    jnp.dot(normed, output_weight_ref[...], preferred_element_type=jnp.float32)
-                    + items_ref[p].astype(jnp.float32)
-                ).astype(jnp.bfloat16)
-                hidden = silu(
-                    jnp.dot(merged, hidden_weight_ref[...], preferred_element_type=jnp.float32)
-                ).astype(jnp.bfloat16)
-                logits_ref[lane, part * requests + i, p] = lax.dot_general(
-                    score_weight_ref[...],
-                    hidden,
-                    (((1,), (1,)), ((), ())),
-                    preferred_element_type=jnp.float32,
-                )
+
+        @pl.when(b == 0)
+        def _():
+            settle((output_piece, hidden_piece))
+
+        @pl.loop(0, chunks)
+        def _(r):
+            i = b * chunks + r
+            merged = (
+                jnp.dot(normed_ref[r], output_weight_ref[...], preferred_element_type=jnp.float32)
+                + items_ref[...].reshape(PARTS * rows, width).astype(jnp.float32)
+            ).astype(jnp.bfloat16)
+            hidden = silu(
+                jnp.dot(merged, hidden_weight_ref[...], preferred_element_type=jnp.float32)
+            ).astype(jnp.bfloat16)
+            logits = lax.dot_general(
+                score_weight_ref[...],
+                hidden,
+                (((1,), (1,)), ((), ())),
+                preferred_element_type=jnp.float32,
+            )
+            for p in range(PARTS):
+                logits_ref[lane, part * requests + i, p] = logits[:, p * rows : (p + 1) * rows]
 
             for k, target in enumerate(others):
                 logit_copy(i, k, target, shard).start()
@@ -536,6 +561,7 @@
             pltpu.VMEM((PARTS * rows, width), jnp.float32),
             pltpu.VMEM((2, history_total, span), jnp.bfloat16),
             pltpu.VMEM((chunks, chunks, PARTS * rows, span), jnp.float32),
+            pltpu.VMEM((chunks, PARTS * rows, width), jnp.bfloat16),
             pltpu.SemaphoreType.DMA((pieces, groups // 2)),
             pltpu.SemaphoreType.DMA((pieces, groups)),
             pltpu.SemaphoreType.DMA((pieces, groups // 2)),

time: 102 us -> 98 us (0.961)
  Pallas kernels: 98.5 us -> 94.1 us
    pallas_call x1, Pallas kernels: 98.5 us -> 94.1 us  [pair_logits(): pl.pallas_call(functools.partial(pair_kernel, groups, shards), out_shape=...]
where the time goes in v2:
time: 98 us; the launch traced here: 97.7 us
  Pallas kernels  94.1 us (96%)
  local copies, waits for them, and re-layouts  2.51 us (3%)
  other arithmetic  1 us (1%)
    pallas_call x1, Pallas kernels, pair_logits(): pl.pallas_call(functools.partial(pair_kernel, groups, shards), out_shape=...  94.1 us

profile of v2, /device:TPU:0, one launch (start us, length us, event | category | flops | bytes accessed | tf_op | source)
XLA Modules:
  0.0 97.7 jit_solution(2432366435914736318)
XLA Ops:
  0.0 94.1 %shard_map.127 = f32[2,8,2,2,512]{4,3,2,1,0:T(2,128)} custom-call(s32[8]{0:T(128)} %length_ref.1, bf16[8,64,1024]{2,1,0:T(8,128)(2,1)} %history_ref.1, bf16[512,1024]{1,0:T(8,128)(2,1)} %bitcast.21, bf16[128,2048]{1,0:T(8,128)(2,1)} %history_shard_ref.1, bf16[128,2048]{1,0:T(8,128)(2,1)} %candidate_shard_ref.1, bf16[128,1024]{1,0:T(8,128)(2,1)} %output_shard_ref.1, ...), custom_call_target="tpu_custom_call" | custom-call | tf_op jit(solution)/shard_map/pallas_call | solution.py:541
  94.1 1.0 %reshape.81 = f32[2,8,2,2,4,128]{5,4,3,2,1,0:T(4,128)S(1)} reshape(f32[2,8,2,2,512]{4,3,2,1,0:T(2,128)} %shard_map.127) | data formatting | bytes 262144 | tf_op jit(solution)/shard_map/reshape | solution.py:593
  95.1 0.0 copy-start.1
  95.1 0.0 copy-start.2
  95.2 0.6 copy-done.1
  95.8 0.0 copy-done.2
  95.8 0.1 constant_dynamic-slice_fusion
  95.9 0.1 broadcast_compare_fusion
  96.0 0.0 copy-start
  96.0 0.2 select_reduce_fusion.1
  96.2 0.1 add.56
  96.3 0.0 copy-start.3
  96.3 0.4 copy-done
  96.8 0.2 copy-done.3
  97.0 0.7 fusion.1
  (5 shorter events, 0.0 us)
Async XLA Ops:
  95.1 0.7 copy-start.1
  95.1 0.7 copy-start.2
  96.0 0.8 copy-start
  96.3 0.7 copy-start.3

commit v3 on v2

--- a/solution.py
+++ b/solution.py
@@ -13,6 +13,7 @@
 EPSILON = 1e-05
 AGE_SCALE = 48.0
 PARTS = 2
+LOGIT_SENDS = 2
 
 
 def silu(value):
@@ -27,28 +28,33 @@
     groups,
     shards,
     length_ref,
+    count_ref,
+    block_shard_ref,
+    block_index_ref,
     history_ref,
     item_shard_ref,
     history_shard_ref,
     candidate_shard_ref,
     output_shard_ref,
     hidden_shard_ref,
+    ages_ref,
     gain_ref,
     score_weight_ref,
-    logits_ref,
+    scores_ref,
     events_ref,
     items_ref,
-    query_weight_ref,
-    key_weight_ref,
-    value_weight_ref,
+    chunk_weight_ref,
     gate_weight_ref,
-    output_weight_ref,
-    hidden_weight_ref,
+    last_weight_ref,
     query_ref,
     gate_ref,
     pairs_ref,
     attended_ref,
     normed_ref,
+    logits_ref,
+    decay_ref,
+    limit_ref,
+    picked_ref,
     weight_send,
     weight_recv,
     pass_send,
@@ -71,7 +77,8 @@
     part, lane = lax.div(shard, lanes), lax.rem(shard, lanes)
     mate = lax.rem(shard + lanes, shards)
     requests, history_total = events_ref.shape[:2]
-    chunks, _, span = query_weight_ref.shape
+    chunks, _, span = query_ref.shape
+    batch_sends = chunks // LOGIT_SENDS
     batches = requests // chunks
     rows = item_shard_ref.shape[0]
     head = width // HEADS
@@ -101,51 +108,17 @@
     def columns(start):
         return pl.ds(pl.multiple_of(start, span), span)
 
-    item_piece = (
-        0,
-        items_ref.at[1 - part, item_rows(group)],
-        lambda source: items_ref.at[1 - part, item_rows(source)],
-    )
-
-    def chunk_pieces(c):
-        return (
-            (
-                1 + 3 * c,
-                candidate_shard_ref.at[:, columns(c * span)],
-                lambda source: query_weight_ref.at[c, rows_of(source)],
-            ),
-            (
-                2 + 3 * c,
-                history_shard_ref.at[:, columns(c * span)],
-                lambda source: key_weight_ref.at[c, rows_of(source)],
-            ),
-            (
-                3 + 3 * c,
-                history_shard_ref.at[:, columns(width + c * span)],
-                lambda source: value_weight_ref.at[c, rows_of(source)],
-            ),
-        )
-
-    gate_piece = (
-        1 + 3 * chunks,
-        candidate_shard_ref.at[:, width:],
-        lambda source: gate_weight_ref.at[rows_of(source)],
-    )
-    output_piece = (
-        2 + 3 * chunks,
-        output_shard_ref,
-        lambda source: output_weight_ref.at[rows_of(source)],
-    )
-    hidden_piece = (
-        3 + 3 * chunks,
-        hidden_shard_ref,
-        lambda source: hidden_weight_ref.at[rows_of(source)],
-    )
+    item_piece = (0, lambda source: items_ref.at[1 - part, item_rows(source)])
+    gate_piece = (1, lambda source: gate_weight_ref.at[rows_of(source)])
+    last_piece = (2, lambda source: last_weight_ref.at[rows_of(source)])
+
+    def chunk_piece(c):
+        return (3 + c, lambda source: chunk_weight_ref.at[c, rows_of(source)])
 
     def weight_copy(piece, k, target, source):
-        w, own, place = piece
-        return pltpu.make_async_remote_copy(
-            src_ref=own,
+        w, place = piece
+        return pltpu.make_async_remote_copy(
+            src_ref=place(source),
             dst_ref=place(source),
             send_sem=weight_send.at[w, k],
             recv_sem=weight_recv.at[w, source],
@@ -154,7 +127,7 @@
         )
 
     def pass_copy(piece, k, source):
-        w, _, place = piece
+        w, place = piece
         return pltpu.make_async_remote_copy(
             src_ref=place(source),
             dst_ref=place(source),
@@ -165,7 +138,7 @@
         )
 
     def turn_copy(piece, k):
-        w, _, place = piece
+        w, place = piece
         source = beside[k] + core * (across - beside[k])
         target = across + core * (beside[k] - across)
         return pltpu.make_async_remote_copy(
@@ -177,9 +150,28 @@
             device_id_type=MESH,
         )
 
-    def own_piece(piece):
-        w, own, place = piece
-        return pltpu.make_async_copy(own, place(group), own_sem.at[w])
+    def own_parts():
+        own = rows_of(group)
+        parts = [(item_shard_ref, items_ref.at[part])]
+        for c in range(chunks):
+            for k, (shard_ref, start) in enumerate(
+                ((candidate_shard_ref, 0), (history_shard_ref, 0), (history_shard_ref, width))
+            ):
+                parts.append(
+                    (
+                        shard_ref.at[:, pl.ds(start + c * span, span)],
+                        chunk_weight_ref.at[c, own, pl.ds(k * span, span)],
+                    )
+                )
+        parts.append((candidate_shard_ref.at[:, pl.ds(width, width)], gate_weight_ref.at[own]))
+        parts.append((output_shard_ref, last_weight_ref.at[own, pl.ds(0, width)]))
+        parts.append(
+            (hidden_shard_ref, last_weight_ref.at[own, pl.ds(width, hidden_shard_ref.shape[1])])
+        )
+        return [
+            pltpu.make_async_copy(source, target, own_sem.at[k])
+            for k, (source, target) in enumerate(parts)
+        ]
 
     def send(pieces):
         for piece in pieces:
@@ -235,9 +227,6 @@
             device_id_type=MESH,
         )
 
-    def own_items():
-        return pltpu.make_async_copy(item_shard_ref, items_ref.at[part], own_sem.at[0])
-
     def event_copy(i, k, target, source):
         return pltpu.make_async_remote_copy(
             src_ref=history_ref.at[lax.div(target, lanes) * requests + i],
@@ -272,23 +261,23 @@
             own_event_sem.at[i],
         )
 
-    def logit_copy(i, k, target, source):
-        place = logits_ref.at[lax.rem(source, lanes), lax.div(source, lanes) * requests + i]
+    def logit_copy(first, k, target, source):
+        place = logits_ref.at[
+            lax.rem(source, lanes), pl.ds(lax.div(source, lanes) * requests + first, batch_sends)
+        ]
+        step = lax.div(first, batch_sends)
         return pltpu.make_async_remote_copy(
             src_ref=place,
             dst_ref=place,
-            send_sem=logit_send.at[i, k],
-            recv_sem=logit_recv.at[i, source],
+            send_sem=logit_send.at[step, k],
+            recv_sem=logit_recv.at[step, source],
             device_id={"cand": target},
             device_id_type=MESH,
         )
 
-    own_items().start()
-    for c in range(chunks):
-        for piece in chunk_pieces(c):
-            own_piece(piece).start()
-    for piece in (gate_piece, output_piece, hidden_piece):
-        own_piece(piece).start()
+    own = own_parts()
+    for copy in own:
+        copy.start()
 
     barrier = pltpu.get_barrier_semaphore()
     for target in (*near, partner):
@@ -297,18 +286,18 @@
         pl.semaphore_signal(barrier, inc=1, device_id={"cand": target}, device_id_type=MESH)
     pl.semaphore_wait(barrier, len(near) + 1 + len(others))
 
-    late = {chunks: (gate_piece,), chunks + 1: (output_piece, hidden_piece)}
+    late = {chunks: gate_piece, chunks + 1: last_piece}
 
     def at_level(action, level):
         @pl.when(level < chunks)
         def _():
-            action(chunk_pieces(level))
-
-        for edge, pieces in late.items():
+            action((chunk_piece(level),))
+
+        for edge, piece in late.items():
 
             @pl.when(level == edge)
             def _():
-                action(pieces)
+                action((piece,))
 
     def send_events(i):
         for k, target in enumerate(others):
@@ -319,37 +308,38 @@
 
         own_event(i).start()
 
-    send(chunk_pieces(0))
+    for copy in own:
+        copy.wait()
+    send((chunk_piece(0),))
     cross_copy().start()
-    send(chunk_pieces(1))
+    send((chunk_piece(1),))
 
     @pl.loop(0, requests)
     def _(i):
         send_events(i)
 
-    turn(chunk_pieces(0))
-    at_level(send, 2)
+    decay_ref[...] = jnp.exp(-ages_ref[...].astype(jnp.float32) / AGE_SCALE)
+
+    for q in range(count_ref.shape[0]):
+        limit_ref[q : q + 1] = jnp.full((1, limit_ref.shape[1]), count_ref[q], jnp.int32)
+
+    turn((chunk_piece(0),))
     cross_arrival().wait_recv()
     send((item_piece,))
-    turn(chunk_pieces(1))
-    own_items().wait()
-    for c in range(chunks):
-        for piece in chunk_pieces(c):
-            own_piece(piece).wait()
-    for piece in (gate_piece, output_piece, hidden_piece):
-        own_piece(piece).wait()
+    at_level(send, 2)
+    turn((chunk_piece(1),))
     turn((item_piece,))
     settle((item_piece,))
 
     def enter_chunk(d):
         at_level(send, d + 3)
-        settle(chunk_pieces(d))
+        settle((chunk_piece(d),))
         query_ref[d] = (
             half_scale
             * silu(
                 jnp.dot(
                     items_ref[...].reshape(PARTS * rows, width),
-                    query_weight_ref[d],
+                    chunk_weight_ref[d, :, :span],
                     preferred_element_type=jnp.float32,
                 )
             )
@@ -381,25 +371,38 @@
         length = length_ref[part * requests + i]
         events = events_ref[i]
         pairs_ref[0] = silu(
-            jnp.dot(events, key_weight_ref[c], preferred_element_type=jnp.float32)
+            jnp.dot(
+                events,
+                chunk_weight_ref[c, :, span : 2 * span],
+                preferred_element_type=jnp.float32,
+            )
         ).astype(jnp.bfloat16)
         live = lax.broadcasted_iota(jnp.int32, (history_total, span), 0) < length
         pairs_ref[1] = jnp.where(
             live,
-            silu(jnp.dot(events, value_weight_ref[c], preferred_element_type=jnp.float32)),
+            silu(
+                jnp.dot(
+                    events,
+                    chunk_weight_ref[c, :, 2 * span :],
+                    preferred_element_type=jnp.float32,
+                )
+            ),
             0.0,
         ).astype(jnp.bfloat16)
-        for h in range(span // head):
-            lanes_of = slice(h * head, (h + 1) * head)
-            scores = lax.dot_general(
-                query_ref[c, :, lanes_of],
-                pairs_ref[0, :, lanes_of],
+        heads = [slice(h * head, (h + 1) * head) for h in range(span // head)]
+        scores = [
+            lax.dot_general(
+                query_ref[c, :, h],
+                pairs_ref[0, :, h],
                 (((1,), (1,)), ((), ())),
                 preferred_element_type=jnp.float32,
             )
-            mixed = (scores + scores * jnp.tanh(scores)).astype(jnp.bfloat16)
-            attended_ref[r, c, :, lanes_of] = jnp.dot(
-                mixed, pairs_ref[1, :, lanes_of], preferred_element_type=jnp.float32
+            for h in heads
+        ]
+        mixed = [(value + value * jnp.tanh(value)).astype(jnp.bfloat16) for value in scores]
+        for h, value in zip(heads, mixed):
+            attended_ref[r, c, :, h] = jnp.dot(
+                value, pairs_ref[1, :, h], preferred_element_type=jnp.float32
             )
 
     def run_batch(b):
@@ -465,17 +468,17 @@
 
         @pl.when(b == 0)
         def _():
-            settle((output_piece, hidden_piece))
+            settle((last_piece,))
 
         @pl.loop(0, chunks)
         def _(r):
             i = b * chunks + r
             merged = (
-                jnp.dot(normed_ref[r], output_weight_ref[...], preferred_element_type=jnp.float32)
+                jnp.dot(normed_ref[r], last_weight_ref[:, :width], preferred_element_type=jnp.float32)
                 + items_ref[...].reshape(PARTS * rows, width).astype(jnp.float32)
             ).astype(jnp.bfloat16)
             hidden = silu(
-                jnp.dot(merged, hidden_weight_ref[...], preferred_element_type=jnp.float32)
+                jnp.dot(merged, last_weight_ref[:, width:], preferred_element_type=jnp.float32)
             ).astype(jnp.bfloat16)
             logits = lax.dot_general(
                 score_weight_ref[...],
@@ -483,11 +486,15 @@
                 (((1,), (1,)), ((), ())),
                 preferred_element_type=jnp.float32,
             )
-            for p in range(PARTS):
-                logits_ref[lane, part * requests + i, p] = logits[:, p * rows : (p + 1) * rows]
-
-            for k, target in enumerate(others):
-                logit_copy(i, k, target, shard).start()
+            for n in range(PARTS * rows // BLOCK):
+                logits_ref[lane, part * requests + i, n // (rows // BLOCK), n % (rows // BLOCK)] = (
+                    logits[:, n * BLOCK : (n + 1) * BLOCK]
+                )
+
+            @pl.when(lax.rem(r, batch_sends) == batch_sends - 1)
+            def _():
+                for k, target in enumerate(others):
+                    logit_copy(i + 1 - batch_sends, k, target, shard).start()
 
     if batches == 1:
         run_batch(0)
@@ -498,11 +505,11 @@
             run_batch(b)
 
     cross_copy().wait_send()
-    finish((item_piece, gate_piece, output_piece, hidden_piece))
+    finish((item_piece, gate_piece, last_piece))
 
     @pl.loop(0, chunks)
     def _(c):
-        finish(chunk_pieces(c))
+        finish((chunk_piece(c),))
 
     @pl.loop(0, requests)
     def _(i):
@@ -518,14 +525,34 @@
             def _():
                 relay_copy(i, k).wait_send()
 
+    @pl.loop(0, requests // batch_sends)
+    def _(step):
         for k, target in enumerate(others):
-            logit_copy(i, k, target, shard).wait_send()
-            logit_copy(i, k, target, target).wait_recv()
-
-
-def pair_logits(
-    history, length, items, history_weight, candidate_weight, output_weight, hidden_weight, gain,
-    score_weight,
+            logit_copy(step * batch_sends, k, target, shard).wait_send()
+            logit_copy(step * batch_sends, k, target, target).wait_recv()
+
+    all_requests, max_blocks = block_shard_ref.shape
+    per_scorer = max_blocks // shards
+
+    for q in range(all_requests):
+        for j in range(per_scorer):
+            slot = shard * per_scorer + j
+            source = block_shard_ref[q, slot]
+            found = logits_ref[
+                lax.rem(source, lanes), q, lax.div(source, lanes), block_index_ref[q, slot]
+            ]
+            for n in range(score_weight_ref.shape[0]):
+                picked_ref[n, q : q + 1, j * BLOCK : (j + 1) * BLOCK] = found[n : n + 1]
+
+    row_number = shard * (per_scorer * BLOCK) + lax.broadcasted_iota(jnp.int32, ages_ref.shape, 1)
+    decay = decay_ref[...]
+    blended = decay * picked_ref[0] + (1.0 - decay) * picked_ref[1]
+    scores_ref[...] = jnp.where(row_number < limit_ref[...], blended, 0.0)
+
+
+def pair_scores(
+    length, count, block_shard, block_index, history, items, history_weight, candidate_weight,
+    output_weight, hidden_weight, ages, gain, score_weight,
 ):
     all_requests, own_events, width = history.shape
     rows = items.shape[0]
@@ -535,33 +562,37 @@
     chunks = HEADS // 2
     span = width // chunks
     depth = history_weight.shape[0] * groups
-    pieces = 4 + 3 * chunks
+    pieces = 3 + chunks
+    small = pl.BlockSpec(memory_space=pltpu.SMEM)
     whole = pl.BlockSpec(memory_space=pltpu.VMEM)
     apart = pl.BlockSpec(memory_space=pl.ANY)
+    sends = requests * LOGIT_SENDS // chunks
     return pl.pallas_call(
         functools.partial(pair_kernel, groups, shards),
-        out_shape=jax.ShapeDtypeStruct(
-            (shards // PARTS, all_requests, PARTS, score_weight.shape[0], rows), jnp.float32
-        ),
-        in_specs=[
-            pl.BlockSpec(memory_space=pltpu.SMEM),
-            apart, apart, apart, apart, apart, apart, whole, whole,
-        ],
+        out_shape=jax.ShapeDtypeStruct(ages.shape, jnp.float32),
+        in_specs=[small] * 4 + [apart] * 6 + [whole] * 3,
         out_specs=whole,
         scratch_shapes=[
             pltpu.VMEM((requests, history_total, width), jnp.bfloat16),
             pltpu.VMEM((PARTS, rows, width), jnp.bfloat16),
-            pltpu.VMEM((chunks, depth, span), jnp.bfloat16),
-            pltpu.VMEM((chunks, depth, span), jnp.bfloat16),
-            pltpu.VMEM((chunks, depth, span), jnp.bfloat16),
+            pltpu.VMEM((chunks, depth, 3 * span), jnp.bfloat16),
             pltpu.VMEM((depth, width), jnp.bfloat16),
-            pltpu.VMEM((depth, width), jnp.bfloat16),
-            pltpu.VMEM((depth, hidden_weight.shape[1]), jnp.bfloat16),
+            pltpu.VMEM((depth, width + hidden_weight.shape[1]), jnp.bfloat16),
             pltpu.VMEM((chunks, PARTS * rows, span), jnp.bfloat16),
             pltpu.VMEM((PARTS * rows, width), jnp.float32),
             pltpu.VMEM((2, history_total, span), jnp.bfloat16),
             pltpu.VMEM((chunks, chunks, PARTS * rows, span), jnp.float32),
             pltpu.VMEM((chunks, PARTS * rows, width), jnp.bfloat16),
+            pltpu.VMEM(
+                (
+                    shards // PARTS, all_requests, PARTS, rows // BLOCK, score_weight.shape[0],
+                    BLOCK,
+                ),
+                jnp.float32,
+            ),
+            pltpu.VMEM(ages.shape, jnp.float32),
+            pltpu.VMEM(ages.shape, jnp.int32),
+            pltpu.VMEM((score_weight.shape[0], *ages.shape), jnp.float32),
             pltpu.SemaphoreType.DMA((pieces, groups // 2)),
             pltpu.SemaphoreType.DMA((pieces, groups)),
             pltpu.SemaphoreType.DMA((pieces, groups // 2)),
@@ -570,48 +601,18 @@
             pltpu.SemaphoreType.DMA,
             pltpu.SemaphoreType.DMA((requests, shards + 1)),
             pltpu.SemaphoreType.DMA((requests, shards)),
-            pltpu.SemaphoreType.DMA((requests, shards)),
-            pltpu.SemaphoreType.DMA((requests, shards)),
-            pltpu.SemaphoreType.DMA((pieces,)),
+            pltpu.SemaphoreType.DMA((sends, shards)),
+            pltpu.SemaphoreType.DMA((sends, shards)),
+            pltpu.SemaphoreType.DMA((4 + 3 * chunks,)),
             pltpu.SemaphoreType.DMA((requests,)),
         ],
         compiler_params=pltpu.CompilerParams(
             collective_id=0, has_side_effects=True, vmem_limit_bytes=60 * 1024 * 1024
         ),
     )(
-        length, history, items, history_weight, candidate_weight, output_weight, hidden_weight,
-        gain, score_weight,
+        length, count, block_shard, block_index, history, items, history_weight, candidate_weight,
+        output_weight, hidden_weight, ages, gain, score_weight,
     )
-
-
-def blend(logits, candidate_count, block_shard, block_index, item_ages, item_blocks):
-    shards = lax.axis_size("cand")
-    mine = lax.axis_index("cand")
-    lanes = shards // PARTS
-    requests, max_blocks = block_shard.shape
-    per_scorer = max_blocks // shards
-    logits = logits.reshape(lanes, requests, PARTS, -1, item_blocks, BLOCK)
-    ids = lax.dynamic_slice_in_dim(
-        block_shard * item_blocks + block_index, mine * per_scorer, per_scorer, 1
-    )
-    names = (
-        jnp.arange(shards * item_blocks, dtype=jnp.int32)
-        .reshape(PARTS, lanes, item_blocks)
-        .transpose(1, 0, 2)[:, None, :, None, :, None]
-    )
-    picked = ids[None, :, None, :, None, None] == names
-    first, second = (
-        jnp.sum(jnp.where(picked, logits[:, :, :, None, c], 0.0), axis=(0, 2, 4)) for c in (0, 1)
-    )
-    decays = jnp.exp(
-        -item_ages.astype(jnp.float32).reshape(requests, per_scorer, BLOCK) / AGE_SCALE
-    )
-    blended = decays * first + (1.0 - decays) * second
-    row_number = (mine * per_scorer + jnp.arange(per_scorer, dtype=jnp.int32))[
-        None, :, None
-    ] * BLOCK + jnp.arange(BLOCK, dtype=jnp.int32)[None, None, :]
-    kept_rows = row_number < candidate_count[:, None, None]
-    return jnp.where(kept_rows, blended, 0.0).reshape(requests, per_scorer * BLOCK)
 
 
 def local(
@@ -629,19 +630,21 @@
     norm_gain,
     score_weight,
 ):
-    item_blocks = item_table.shape[0]
-    logits = pair_logits(
+    return pair_scores(
+        history_length,
+        candidate_count,
+        block_shard,
+        block_index,
         history,
-        history_length,
         item_table.reshape(-1, item_table.shape[2]),
         history_weight,
         candidate_weight,
         output_weight,
         hidden_weight,
+        item_ages,
         norm_gain[None, :],
         score_weight,
     )
-    return blend(logits, candidate_count, block_shard, block_index, item_ages, item_blocks)
 
 
 def solution(mesh):

time: 98 us -> 93.2 us (0.951)
  Pallas kernels: 94.1 us -> 91.6 us
  local copies, waits for them, and re-layouts: 2.51 us -> 1.38 us
  other arithmetic: 1 us -> 0 us
    pallas_call x1, Pallas kernels: 94.1 us -> 91.6 us  [pair_scores(): pl.pallas_call(functools.partial(pair_kernel, groups, shards), out_shape=...]
    reshape x1 -> x0, local copies, waits for them, and re-layouts: 1.03 us -> none  [blend(): logits = logits.reshape(lanes, requests, PARTS, -1, item_blocks, BLOCK)]
where the time goes in v3:
time: 93.2 us; the launch traced here: 93 us
  Pallas kernels  91.6 us (98%)
  local copies, waits for them, and re-layouts  1.38 us (1%)
    pallas_call x1, Pallas kernels, pair_scores(): pl.pallas_call(functools.partial(pair_kernel, groups, shards), out_shape=...  91.6 us

profile of v3, /device:TPU:0, one launch (start us, length us, event | category | flops | bytes accessed | tf_op | source)
XLA Modules:
  0.0 93.0 jit_solution(12083609143913650826)
XLA Ops:
  0.0 91.6 %shard_map.127 = f32[8,1024]{1,0:T(8,128)} custom-call(s32[8]{0:T(128)} %length_ref.1, s32[8]{0:T(128)} %count_ref.1, s32[8,32]{1,0:T(8,128)} %block_shard_ref.1, s32[8,32]{1,0:T(8,128)} %block_index_ref.1, bf16[8,64,1024]{2,1,0:T(8,128)(2,1)} %history_ref.1, bf16[512,1024]{1,0:T(8,128)(2,1)} %bitcast.2, bf16[128,2048]{1,0:T(8,128)(2,1)} %history_shard_ref.1, ...), custom_call_target="tpu_custom_call" | custom-call | tf_op jit(solution)/shard_map/pallas_call | solution.py:570
  91.6 1.4 %copy.15 = f32[8,1024]{1,0:T(8,128)} copy(f32[8,1024]{1,0:T(8,128)} %shard_map.127) | data formatting | bytes 65536

commit v4 on v3

--- a/solution.py
+++ b/solution.py
@@ -14,6 +14,8 @@
 AGE_SCALE = 48.0
 PARTS = 2
 LOGIT_SENDS = 2
+ENTER = {1: [('send', 4)], 2: [('send', 5)]}
+MIDDLE = {0: [('hand', 1), ('turn', 2)], 1: [('hand', 2), ('turn', 3)], 2: [('hand', 3), ('turn', 4)], 3: [('hand', 4), ('turn', 5)]}
 
 
 def silu(value):
@@ -190,11 +192,13 @@
             for k, source in enumerate(near):
                 pass_copy(piece, k, source).start()
 
-    def settle(pieces):
+    def hand(pieces):
         for piece in pieces:
             arrive(piece, diagonal)
             for k, source in enumerate(diagonal):
                 pass_copy(piece, len(near) + k, source).start()
+
+    def collect(pieces):
         for piece in pieces:
             arrive(piece, (partner, *partner_core))
 
@@ -286,18 +290,21 @@
         pl.semaphore_signal(barrier, inc=1, device_id={"cand": target}, device_id_type=MESH)
     pl.semaphore_wait(barrier, len(near) + 1 + len(others))
 
-    late = {chunks: gate_piece, chunks + 1: last_piece}
-
-    def at_level(action, level):
-        @pl.when(level < chunks)
-        def _():
-            action((chunk_piece(level),))
-
-        for edge, piece in late.items():
-
-            @pl.when(level == edge)
-            def _():
-                action((piece,))
+    late = {-1: item_piece, chunks: gate_piece, chunks + 1: last_piece}
+
+    def piece_at(level):
+        return late[level] if level in late else chunk_piece(level)
+
+    def run_steps(steps):
+        for action, level in steps:
+            {"send": send, "turn": turn, "hand": hand}[action]((piece_at(level),))
+
+    def at_chunk(table, d):
+        for edge, steps in table.items():
+
+            @pl.when(d == edge)
+            def _():
+                run_steps(steps)
 
     def send_events(i):
         for k, target in enumerate(others):
@@ -319,21 +326,22 @@
         send_events(i)
 
     decay_ref[...] = jnp.exp(-ages_ref[...].astype(jnp.float32) / AGE_SCALE)
-
     for q in range(count_ref.shape[0]):
         limit_ref[q : q + 1] = jnp.full((1, limit_ref.shape[1]), count_ref[q], jnp.int32)
-
     turn((chunk_piece(0),))
     cross_arrival().wait_recv()
     send((item_piece,))
-    at_level(send, 2)
+    send((chunk_piece(2),))
     turn((chunk_piece(1),))
+    hand((chunk_piece(0),))
     turn((item_piece,))
-    settle((item_piece,))
+    hand((item_piece,))
+    send((chunk_piece(3),))
+    collect((item_piece,))
 
     def enter_chunk(d):
-        at_level(send, d + 3)
-        settle((chunk_piece(d),))
+        at_chunk(ENTER, d)
+        collect((chunk_piece(d),))
         query_ref[d] = (
             half_scale
             * silu(
@@ -426,7 +434,7 @@
 
             @pl.when((k == d) & (b == 0))
             def _():
-                at_level(turn, d + 2)
+                at_chunk(MIDDLE, d)
 
             @pl.when(k == d)
             def _():
@@ -436,7 +444,8 @@
 
         @pl.when(b == 0)
         def _():
-            settle((gate_piece,))
+            hand((last_piece,))
+            collect((gate_piece,))
             gate_ref[...] = (
                 silu(
                     jnp.dot(
@@ -448,15 +457,12 @@
                 * gain_ref[...]
             )
 
-        @pl.loop(0, chunks)
-        def _(r):
+        def norm(r):
             length = jnp.full(
                 (1, 1), length_ref[part * requests + b * chunks + r], jnp.int32
             ).astype(jnp.float32)
-
-            @pl.loop(0, PARTS)
-            def _(p):
-                tile = pl.ds(pl.multiple_of(p * rows, rows), rows)
+            for p in range(2 * PARTS):
+                tile = pl.ds(p * rows // 2, rows // 2)
                 attended = jnp.concatenate(
                     [attended_ref[r, c, tile] for c in range(chunks)], axis=-1
                 )
@@ -466,13 +472,16 @@
                     center * lax.rsqrt(spread + EPSILON * length * length) * gate_ref[tile]
                 ).astype(jnp.bfloat16)
 
+        norm(0)
+
         @pl.when(b == 0)
         def _():
-            settle((last_piece,))
-
-        @pl.loop(0, chunks)
-        def _(r):
+            collect((last_piece,))
+
+        for r in range(chunks):
             i = b * chunks + r
+            if r + 1 < chunks:
+                norm(r + 1)
             merged = (
                 jnp.dot(normed_ref[r], last_weight_ref[:, :width], preferred_element_type=jnp.float32)
                 + items_ref[...].reshape(PARTS * rows, width).astype(jnp.float32)
@@ -491,8 +500,7 @@
                     logits[:, n * BLOCK : (n + 1) * BLOCK]
                 )
 
-            @pl.when(lax.rem(r, batch_sends) == batch_sends - 1)
-            def _():
+            if r % batch_sends == batch_sends - 1:
                 for k, target in enumerate(others):
                     logit_copy(i + 1 - batch_sends, k, target, shard).start()
 

time: 93.2 us -> 89.2 us (0.957)
  Pallas kernels: 91.6 us -> 87.5 us
    pallas_call x1, Pallas kernels: 91.6 us -> 87.5 us  [pair_scores(): pl.pallas_call(functools.partial(pair_kernel, groups, shards), out_shape=...]
where the time goes in v4:
time: 89.2 us; the launch traced here: 88.9 us
  Pallas kernels  87.5 us (98%)
  local copies, waits for them, and re-layouts  1.38 us (2%)
    pallas_call x1, Pallas kernels, pair_scores(): pl.pallas_call(functools.partial(pair_kernel, groups, shards), out_shape=...  87.5 us

profile of v4, /device:TPU:0, one launch (start us, length us, event | category | flops | bytes accessed | tf_op | source)
XLA Modules:
  0.0 88.9 jit_solution(2879240911690121356)
XLA Ops:
  0.0 87.5 %shard_map.127 = f32[8,1024]{1,0:T(8,128)} custom-call(s32[8]{0:T(128)} %length_ref.1, s32[8]{0:T(128)} %count_ref.1, s32[8,32]{1,0:T(8,128)} %block_shard_ref.1, s32[8,32]{1,0:T(8,128)} %block_index_ref.1, bf16[8,64,1024]{2,1,0:T(8,128)(2,1)} %history_ref.1, bf16[512,1024]{1,0:T(8,128)(2,1)} %bitcast.2, bf16[128,2048]{1,0:T(8,128)(2,1)} %history_shard_ref.1, ...), custom_call_target="tpu_custom_call" | custom-call | tf_op jit(solution)/shard_map/pallas_call | solution.py:578
  87.6 1.4 %copy.15 = f32[8,1024]{1,0:T(8,128)} copy(f32[8,1024]{1,0:T(8,128)} %shard_map.127) | data formatting | bytes 65536

commit v5 on v4

--- a/solution.py
+++ b/solution.py
@@ -440,22 +440,25 @@
             def _():
                 enter_request(i)
 
+            @pl.when((t + 2 == chunks * chunks) & (b == 0))
+            def _():
+                collect((gate_piece,))
+                gate_ref[...] = (
+                    silu(
+                        jnp.dot(
+                            items_ref[...].reshape(PARTS * rows, width),
+                            gate_weight_ref[...],
+                            preferred_element_type=jnp.float32,
+                        )
+                    )
+                    * gain_ref[...]
+                )
+
             attend(c, r, i)
 
         @pl.when(b == 0)
         def _():
             hand((last_piece,))
-            collect((gate_piece,))
-            gate_ref[...] = (
-                silu(
-                    jnp.dot(
-                        items_ref[...].reshape(PARTS * rows, width),
-                        gate_weight_ref[...],
-                        preferred_element_type=jnp.float32,
-                    )
-                )
-                * gain_ref[...]
-            )
 
         def norm(r):
             length = jnp.full(

time: 89.2 us -> 88.1 us (0.988)
  Pallas kernels: 87.5 us -> 86.5 us
    pallas_call x1, Pallas kernels: 87.5 us -> 86.5 us  [pair_scores(): pl.pallas_call(functools.partial(pair_kernel, groups, shards), out_shape=...]
where the time goes in v5:
time: 88.1 us; the launch traced here: 87.8 us
  Pallas kernels  86.5 us (98%)
  local copies, waits for them, and re-layouts  1.38 us (2%)
    pallas_call x1, Pallas kernels, pair_scores(): pl.pallas_call(functools.partial(pair_kernel, groups, shards), out_shape=...  86.5 us

profile of v5, /device:TPU:0, one launch (start us, length us, event | category | flops | bytes accessed | tf_op | source)
XLA Modules:
  0.0 87.8 jit_solution(1522163497545528047)
XLA Ops:
  0.0 86.5 %shard_map.127 = f32[8,1024]{1,0:T(8,128)} custom-call(s32[8]{0:T(128)} %length_ref.1, s32[8]{0:T(128)} %count_ref.1, s32[8,32]{1,0:T(8,128)} %block_shard_ref.1, s32[8,32]{1,0:T(8,128)} %block_index_ref.1, bf16[8,64,1024]{2,1,0:T(8,128)(2,1)} %history_ref.1, bf16[512,1024]{1,0:T(8,128)(2,1)} %bitcast.2, bf16[128,2048]{1,0:T(8,128)(2,1)} %history_shard_ref.1, ...), custom_call_target="tpu_custom_call" | custom-call | tf_op jit(solution)/shard_map/pallas_call | solution.py:581
  86.5 1.4 %copy.15 = f32[8,1024]{1,0:T(8,128)} copy(f32[8,1024]{1,0:T(8,128)} %shard_map.127) | data formatting | bytes 65536
